TPU v7x, 32 devices: a whole 2x2x4 slice. The times are simulated.
32 devices in a mesh: tile: 8 (over z, y), depth: 4 (over x, core).
Axes of the slice: x: 2, y: 2, z: 4, core: 2. Of those that a mesh axis runs over, the one named last changes fastest.
Arguments:
- positions: float32 [3, 16384], P(None, 'tile'), may hold values from -4 to 4
- log_scales: float32 [3, 16384], P(None, 'tile'), may hold values from -2 to 0
- opacity_logits: float32 [1, 16384], P(None, 'tile'), may hold values from -3 to 1.5
- colors: float32 [3, 16384], P(None, 'tile'), may hold values from 0 to 1
- first_moment: float32 [10, 16384], P(None, 'tile'), may hold values from -3 to 3
- second_moment: float32 [10, 16384], P(None, 'tile'), may hold values from 0.01 to 1
- cameras: float32 [4, 2, 4], replicated, may hold values from -6.4 to 6.4
- background: float32 [3], replicated, may hold values from 0 to 1
- target: float32 [32, 3, 1024], P('tile'), may hold values from 0 to 1
- tile_view: int32 [32], P('tile'), may hold values from 0 to 3
- tile_length: int32 [32], P('tile'), may hold values from 128 to 512
- list_owner: int32 [4, 32, 128, 1], P('depth', 'tile'), may hold values from 0 to 7; in each aligned block of 512 rows (0 to 511, 512 to 1023, ..., all dimensions but the last counted through in order) at most 160 rows name the same one
- list_row: int32 [4, 32, 128], P('depth', 'tile'), may hold values from 0 to 2047
Outputs:
- image: float32 [32, 3, 1024], P('tile')
- new_params: float32 [10, 16384], P(None, 'tile')
- new_first: float32 [10, 16384], P(None, 'tile')
- new_second: float32 [10, 16384], P(None, 'tile')
Inputs may be any that keep to these rules, and one draw needn't show every extreme that they name: `list_owner`: within the entries of one device's block (one depth slab of the tiles of one tile index), no owner is named more than 160 times, a bound that some block reaches.
All inputs are finite; a program needn't handle non-finite values.
Results may differ from a plain program's by a relative error of at most 0.00008.
Values sent between devices are 32-bit elements; how exact they have to be, the bound alone decides.
A program may use at most 64 MiB of HBM per device.

v0:
```python
import jax
import jax.numpy as jnp
from jax import lax
from jax.sharding import PartitionSpec as P

TILE_SIDE = 32


def project(params, cams):
    position = params[0:3]
    variance = jnp.exp(2.0 * params[3:6])
    first_row = cams[:, 0, 0:3].T
    second_row = cams[:, 1, 0:3].T
    center_x = jnp.sum(first_row * position, axis=0) + cams[:, 0, 3] + 0.5 * TILE_SIDE
    center_y = jnp.sum(second_row * position, axis=0) + cams[:, 1, 3] + 0.5 * TILE_SIDE
    cov_xx = jnp.sum(first_row * first_row * variance, axis=0) + 0.3
    cov_xy = jnp.sum(first_row * second_row * variance, axis=0)
    cov_yy = jnp.sum(second_row * second_row * variance, axis=0) + 0.3
    determinant = cov_xx * cov_yy - cov_xy * cov_xy
    return jnp.stack(
        [
            center_x,
            center_y,
            cov_yy / determinant,
            -cov_xy / determinant,
            cov_xx / determinant,
            jax.nn.sigmoid(params[6]),
            params[7],
            params[8],
            params[9],
        ]
    )


def coverage(screen, alive, pixels):
    pixel = jnp.arange(pixels, dtype=jnp.int32)
    pixel_x = (pixel % TILE_SIDE).astype(jnp.float32) + 0.5
    pixel_y = (pixel // TILE_SIDE).astype(jnp.float32) + 0.5
    offset_x = pixel_x[:, None] - screen[0][None, :]
    offset_y = pixel_y[:, None] - screen[1][None, :]
    quadric = (
        screen[2][None, :] * offset_x * offset_x
        + 2.0 * screen[3][None, :] * offset_x * offset_y
        + screen[4][None, :] * offset_y * offset_y
    )
    falloff = jnp.exp(-0.5 * quadric)
    alpha = screen[5][None, :] * falloff * alive[None, :]
    return (offset_x, offset_y, falloff, alpha)


def running_sum(values, triangle):
    rows = values.shape[0]
    width = triangle.shape[0]
    blocks = values.reshape(rows, values.shape[1] // width, width)
    inner = jnp.einsum("pbk,kj->pbj", blocks, triangle, precision=lax.Precision.HIGHEST)
    sums = jnp.sum(blocks, axis=2)
    lead = jnp.cumsum(sums, axis=1) - sums
    return (inner + lead[:, :, None]).reshape(rows, values.shape[1])


def adam_update(param, first, second, gradient):
    new_first = 0.9 * first + 0.1 * gradient
    new_second = 0.999 * second + 0.001 * gradient * gradient
    corrected = new_first / (1.0 - 0.9**10) / (jnp.sqrt(new_second / (1.0 - 0.999**10)) + 1e-08)
    return (param - 0.05 * corrected, new_first, new_second)


def body(
    positions,
    log_scales,
    opacity_logits,
    colors,
    first_moment,
    second_moment,
    cameras,
    background,
    target,
    tile_view,
    tile_length,
    list_owner,
    list_row,
):
    tiles_here = target.shape[0]
    pixels = target.shape[2]
    slab = list_row.shape[2]
    owner_count = lax.axis_size("tile")
    depth_count = lax.axis_size("depth")
    depth_index = lax.axis_index("depth")
    capacity = max(2, 5 * tiles_here * slab // (2 * owner_count))
    highest = lax.Precision.HIGHEST
    params = jnp.concatenate([positions, log_scales, opacity_logits, colors], axis=0)
    owner = list_owner.reshape(-1)
    wanted = list_row.reshape(-1)
    viewed = jnp.repeat(tile_view, slab)
    onehot = (owner[:, None] == jnp.arange(owner_count, dtype=jnp.int32)[None, :]).astype(jnp.int32)
    rank = jnp.sum((jnp.cumsum(onehot, axis=0) - onehot) * onehot, axis=1)
    slot = owner * capacity + rank
    request = (
        jnp.zeros((2, owner_count * capacity), jnp.int32)
        .at[:, slot]
        .set(jnp.stack([wanted, viewed]))
    )
    request = request.reshape(2, owner_count, capacity)
    received = lax.all_to_all(request, "tile", split_axis=1, concat_axis=1, tiled=True)
    rows_in = received[0].reshape(-1)
    views_in = received[1].reshape(-1)
    screen = project(params[:, rows_in], cameras[views_in])
    screen = screen.reshape(9, received.shape[1], received.shape[2])
    fetched = lax.all_to_all(screen, "tile", split_axis=1, concat_axis=1, tiled=True)
    entry = fetched.reshape(9, -1)[:, slot].reshape(9, tiles_here, slab).transpose(1, 0, 2)
    order = jnp.arange(slab, dtype=jnp.int32)
    strict = (order[:, None] < order[None, :]).astype(jnp.float32)
    inclusive = (order[:, None] <= order[None, :]).astype(jnp.float32)

    def forward(args):
        screen, alive = args
        offset_x, offset_y, falloff, alpha = coverage(screen, alive, pixels)
        leak = jnp.log1p(-alpha)
        before = running_sum(leak, strict)
        weight = alpha * jnp.exp(before)
        color = jnp.einsum("ck,pk->cp", screen[6:9], weight, precision=highest)
        return (jnp.sum(leak, axis=1), color)

    def backward(args):
        screen, alive, start_log, start_color, whole, miss = args
        offset_x, offset_y, falloff, alpha = coverage(screen, alive, pixels)
        leak = jnp.log1p(-alpha)
        local = running_sum(leak, strict)
        carried = jnp.exp(start_log)[:, None]
        inside = jnp.exp(local)
        trans = carried * inside
        weight = alpha * trans
        local_weight = alpha * inside
        d_alpha = jnp.zeros_like(alpha)
        for channel in range(3):
            shade = screen[6 + channel][None, :]
            upto = running_sum(local_weight * shade, inclusive)
            behind = whole[channel][:, None] - start_color[channel][:, None] - carried * upto
            d_alpha = d_alpha + miss[channel][:, None] * (trans * shade - behind / (1.0 - alpha))
        d_color = jnp.einsum("cp,pk->ck", miss, weight, precision=highest)
        d_quad = d_alpha * (-0.5 * alpha)
        d_opacity = jnp.sum(d_alpha * falloff * alive[None, :], axis=0)
        d_center_x = jnp.sum(
            d_quad * -2.0 * (screen[2][None, :] * offset_x + screen[3][None, :] * offset_y), axis=0
        )
        d_center_y = jnp.sum(
            d_quad * -2.0 * (screen[3][None, :] * offset_x + screen[4][None, :] * offset_y), axis=0
        )
        d_conic_a = jnp.sum(d_quad * offset_x * offset_x, axis=0)
        d_conic_b = jnp.sum(d_quad * 2.0 * offset_x * offset_y, axis=0)
        d_conic_c = jnp.sum(d_quad * offset_y * offset_y, axis=0)
        return jnp.concatenate(
            [
                jnp.stack([d_center_x, d_center_y, d_conic_a, d_conic_b, d_conic_c, d_opacity]),
                d_color,
            ],
            axis=0,
        )

    quarter = tiles_here // depth_count
    whole_entry = lax.all_to_all(entry, "depth", split_axis=0, concat_axis=2, tiled=True)
    first_tile = depth_index * quarter
    own_length = lax.dynamic_slice_in_dim(tile_length, first_tile, quarter, 0)
    full_place = jnp.arange(slab * depth_count, dtype=jnp.int32)
    own_live = (full_place[None, :] < own_length[:, None]).astype(jnp.float32)
    own_log, own_color = lax.map(forward, (whole_entry, own_live))
    own_image = own_color + jnp.exp(own_log)[:, None, :] * background[None, :, None]
    own_error = own_image - lax.dynamic_slice_in_dim(target, first_tile, quarter, 0)
    zero_log = jnp.zeros_like(own_log)
    zero_color = jnp.zeros_like(own_color)
    own_grad = lax.map(
        backward, (whole_entry, own_live, zero_log, zero_color, own_image, own_error)
    )
    entry_grad = lax.all_to_all(own_grad, "depth", split_axis=2, concat_axis=0, tiled=True)
    image = lax.all_gather(own_image, "depth", axis=0, tiled=True)
    flat_grad = entry_grad.transpose(1, 0, 2).reshape(9, -1)
    outgoing = jnp.zeros((9, owner_count * capacity), jnp.float32).at[:, slot].set(flat_grad)
    outgoing = outgoing.reshape(9, owner_count, capacity)
    incoming = lax.all_to_all(outgoing, "tile", split_axis=1, concat_axis=1, tiled=True)
    rows_in = received[0].reshape(-1)
    views_in = received[1].reshape(-1)
    chosen_cams = cameras[views_in]
    unused, pullback = jax.vjp(lambda chosen: project(chosen, chosen_cams), params[:, rows_in])
    (slot_grad,) = pullback(incoming.reshape(9, -1))
    gradient = jnp.zeros_like(params).at[:, rows_in].add(slot_grad)
    gradient = lax.psum(gradient, "depth")
    new_params, new_first, new_second = adam_update(params, first_moment, second_moment, gradient)
    return (image, new_params, new_first, new_second)


def solution(mesh):
    placed = (
        P(None, "tile"),
        P(None, "tile"),
        P(None, "tile"),
        P(None, "tile"),
        P(None, "tile"),
        P(None, "tile"),
        P(),
        P(),
        P("tile", None, None),
        P("tile"),
        P("tile"),
        P("depth", "tile", None, None),
        P("depth", "tile", None),
    )
    return jax.shard_map(
        body,
        mesh=mesh,
        in_specs=placed,
        out_specs=(P("tile", None, None), P(None, "tile"), P(None, "tile"), P(None, "tile")),
        check_vma=False,
    )
```

profile of v0, /device:TPU:0, one launch (start us, length us, event | category | flops | bytes accessed | tf_op | source)
XLA Modules:
  0.0 199.4 jit_solution(7363935695881023951)
XLA Ops:
  12.3 1.9 scatter_custom_fusion
  15.2 7.3 %all-to-all-start = ((s32[2,8,160]{2,0,1:T(2,128)}), s32[2,8,160]{2,0,1:T(2,128)S(1)}, u32[]{:S(2)}, u32[]{:S(2)}) async-start(s32[2,8,160]{2,0,1:T(2,128)} %copy.152), calls=%async_computation | async-start | bytes 32768 | tf_op jit(solution)/shard_map/all_to_all | solution.py:104
  24.3 4.7 %all-to-all-done = s32[2,8,160]{2,0,1:T(2,128)S(1)} async-done(((s32[2,8,160]{2,0,1:T(2,128)}), s32[2,8,160]{2,0,1:T(2,128)S(1)}, u32[]{:S(2)}, u32[]{:S(2)}) %all-to-all-start) | async-done | bytes 10272 | tf_op jit(solution)/shard_map/all_to_all | solution.py:104
  29.2 4.3 %gather_fusion = f32[1280,2,4]{2,1,0:T(2,128)S(1)} fusion(f32[4,2,4]{2,1,0:T(2,128)S(1)} %copy-done.1, s32[2048]{0:T(1024)S(1)} %pad_clamp_fusion.1), kind=kCustom, calls=%fused_computation | custom fusion | bytes 87040 | tf_op jit(solution)/shard_map/gather | solution.py:107
  35.3 36.3 %slice_reduce_fusion = (f32[1280]{0:T(1024)S(1)}, f32[1280]{0:T(1024)S(1)}) fusion(f32[1280,2,4]{2,1,0:T(2,128)S(1)} %gather_fusion), kind=kLoop, calls=%fused_computation.71 | loop fusion | bytes 20480 | tf_op jit(solution)/shard_map/slice | solution.py:15
  73.4 2.4 %gather_fusion.1 = f32[1280,10]{1,0:T(8,128)S(1)} fusion(f32[10,2048]{0,1:T(8,128)S(1)} %copy.154, s32[2048]{0:T(1024)S(1)} %pad_clamp_fusion), kind=kCustom, calls=%fused_computation.1 | custom fusion | bytes 107520 | tf_op jit(solution)/shard_map/gather | solution.py:107
  78.0 3.5 %all-to-all-start.1 = ((f32[8,1,1440]{2,1,0:T(1,128)}), f32[8,1,1440]{2,1,0:T(1,128)S(1)}, u32[]{:S(2)}, u32[]{:S(2)}) async-start(f32[8,1,1440]{2,1,0:T(1,128)} %reshape.1452), calls=%async_computation.1 | async-start | bytes 98304 | tf_op jit(solution)/shard_map/all_to_all | solution.py:109
  82.2 5.9 %all-to-all-done.1 = f32[8,1,1440]{2,1,0:T(1,128)S(1)} async-done(((f32[8,1,1440]{2,1,0:T(1,128)}), f32[8,1,1440]{2,1,0:T(1,128)S(1)}, u32[]{:S(2)}, u32[]{:S(2)}) %all-to-all-start.1) | async-done | bytes 46112 | tf_op jit(solution)/shard_map/all_to_all | solution.py:109
  91.5 3.3 %all-to-all-start.2 = ((f32[4,9,128]{2,1,0:T(8,128)}), f32[4,9,128]{2,1,0:T(8,128)S(1)}, u32[]{:S(2)}, u32[]{:S(2)}) async-start(f32[4,9,128]{2,1,0:T(8,128)} %bitcast.21), calls=%async_computation.2 | async-start | bytes 65536 | tf_op jit(solution)/shard_map/all_to_all | solution.py:161
  95.5 3.2 %all-to-all-done.2 = f32[4,9,128]{2,1,0:T(8,128)S(1)} async-done(((f32[4,9,128]{2,1,0:T(8,128)}), f32[4,9,128]{2,1,0:T(8,128)S(1)}, u32[]{:S(2)}, u32[]{:S(2)}) %all-to-all-start.2) | async-done | bytes 18464 | tf_op jit(solution)/shard_map/all_to_all | solution.py:161
  98.7 2.0 fusion.28
  100.8 5.9 %multiply_reduce_fusion.3 = (f32[1024,4]{0,1:T(4,128)S(1)}, f32[1024,4]{0,1:T(4,128)S(1)}, f32[1024,4]{0,1:T(4,128)S(1)}, f32[1024,4,128]{0,2,1:T(8,128)S(1)}, f32[1024,4,128]{0,2,1:T(8,128)}) fusion(f32[4,128]{1,0:T(4,128)S(1)} %bitcast.208, f32[4,128]{1,0:T(4,128)S(1)} %bitcast.188, f32[4,128]{1,0:T(4,128)S(1)} %bitcast.185, f32[1024,4]{0,1:T(4,128)S(1)} %sub.316, ...), kind=kOutput, calls=%fused_computation.60 | convolution fusion | flops 823660544 | bytes 4288512 | tf_op jit(solution)/shard_map/while/body/eval_jaxpr/pbk,kj->pbj/dot_general | solution.py:55
  106.7 2.9 %fusion.24 = f32[1024,4,128]{0,2,1:T(8,128)} fusion(f32[1024,4,128]{0,2,1:T(8,128)S(1)} %get-tuple-element.96, f32[4,128]{1,0:T(4,128)S(1)} %bitcast.189), kind=kOutput, calls=%fused_computation.58 | convolution fusion | flops 805847040 | bytes 4196352 | tf_op jit(solution)/shard_map/while/body/eval_jaxpr/pbk,kj->pbj/dot_general | solution.py:55
  109.6 2.9 %fusion.22 = f32[1024,4,128]{0,2,1:T(8,128)} fusion(f32[1024,4,128]{0,2,1:T(8,128)S(1)} %get-tuple-element.96, f32[4,128]{1,0:T(4,128)S(1)} %bitcast.186), kind=kOutput, calls=%fused_computation.55 | convolution fusion | flops 805847040 | bytes 4196352 | tf_op jit(solution)/shard_map/while/body/eval_jaxpr/pbk,kj->pbj/dot_general | solution.py:55
  112.5 1.9 fusion.14
  115.5 1.8 fusion.56
  117.5 6.2 %multiply_multiply_fusion = (f32[1024,4,128]{0,2,1:T(8,128)S(1)}, f32[1024,4,128]{0,2,1:T(8,128)S(1)}) fusion(f32[4,128]{1,0:T(4,128)S(1)} %fusion.74, f32[4,128]{1,0:T(4,128)S(1)} %bitcast.168, f32[4,128]{1,0:T(4,128)S(1)} %bitcast.173, f32[1024]{0:T(1024)S(1)} %get-tuple-element.136, f32[4,128]{1,0:T(4,128)S(1)} %broadcast_multiply_fusion.1, ...), kind=kOutput, calls=%fused_computation.49 | convolution fusion | flops 825245696 | bytes 12701696 | tf_op jit(solution)/shard_map/while/body/eval_jaxpr/pbk,kj->pbj/dot_general | solution.py:55
  123.7 3.8 %fusion.3 = (f32[4,128]{1,0:T(4,128)S(1)}, f32[4,128]{1,0:T(4,128)S(1)}, f32[4,128]{1,0:T(4,128)S(1)}, f32[4,128]{1,0:T(4,128)S(1)}, f32[4,128]{1,0:T(4,128)S(1)}, /*index=5*/f32[4,128]{1,0:T(4,128)S(1)}) fusion(f32[1024,4,128]{0,2,1:T(8,128)S(1)} %get-tuple-element.131, f32[4,128]{1,0:T(4,128)S(1)} %bitcast.162, f32[4,128]{1,0:T(4,128)S(1)} %bitcast.169, ...), kind=kLoop, calls=%fused_computation.29 | loop fusion | flops 17298432 | bytes 4229120 | tf_op jit(solution)/shard_map/while/body/eval_jaxpr/reduce_sum | solution.py:146
  129.4 6.2 %all_to_all.48 = f32[4,1,1152]{2,1,0:T(1,128)S(1)} all-to-all(f32[4,1,1152]{2,1,0:T(1,128)S(1)} %reshape.1454), channel_id=1, replica_groups=mesh['tile'=8,'depth'=4] {'depth'}, dimensions={0} | all-to-all | bytes 36864 | tf_op jit(solution)/shard_map/all_to_all | solution.py:174
  137.0 1.9 scatter_custom_fusion.1
  139.3 9.2 %all_to_all.49 = f32[8,1,1440]{2,1,0:T(1,128)S(1)} all-to-all(f32[8,1,1440]{2,1,0:T(1,128)S(1)} %reshape.1456), channel_id=1, replica_groups=mesh['tile'=8,'depth'=4] {'tile'}, dimensions={0} | all-to-all | bytes 92160 | tf_op jit(solution)/shard_map/all_to_all | solution.py:179
  150.8 9.2 %scatter_custom_fusion.2 = f32[10,2048]{0,1:T(8,128)S(1)} fusion(s32[1280]{0:T(1024)S(1)} %fusion.60, f32[1280,10]{1,0:T(8,128)S(1)} %copy.178, f32[]{:T(128)} %constant.132.clone.1), kind=kCustom, calls=%fused_computation.73 | custom fusion | flops 12800 | bytes 81924 | tf_op jit(solution)/shard_map/scatter-add | solution.py:185
  161.0 5.2 %all-gather.1 = f32[4,3,1024]{2,1,0:T(4,128)S(1)} all-gather(f32[1,3,1024]{2,1,0:T(4,128)S(1)} %get-tuple-element.130), channel_id=2, replica_groups=mesh['tile'=8,'depth'=4] {'depth'}, dimensions={0}, use_global_device_ids=true | all-gather | bytes 61440 | tf_op jit(solution)/shard_map/all_gather | solution.py:175
  166.8 23.9 %all-reduce.8.cloned.1.call-done = f32[10,2048]{1,0:T(8,128)} async-done(((f32[10,2048]{1,0:T(8,128)}), f32[10,2048]{1,0:T(8,128)}) %all-reduce.8.cloned.1.call-update) | async-done | bytes 81936 | tf_op jit(solution)/shard_map/psum | solution.py:186
  (127 shorter events, 29.1 us)
Async XLA Ops:
  7.2 15.3 %copy-start = (f32[4,3,1024]{2,0,1:T(4,128)S(1)}, f32[4,3,1024]{2,0,1:T(4,128)}, u32[]{:S(2)}) copy-start(f32[4,3,1024]{2,0,1:T(4,128)} %param.21) | copy-start | bytes 147460
  7.2 16.6 %copy-start.9 = (s32[4]{0:T(128)S(1)}, s32[4]{0:T(128)}, u32[]{:S(2)}) copy-start(s32[4]{0:T(128)} %param.23) | copy-start | bytes 52
  7.2 22.0 %copy-start.1 = (f32[4,2,4]{2,1,0:T(2,128)S(1)}, f32[4,2,4]{2,1,0:T(2,128)}, u32[]{:S(2)}) copy-start(f32[4,2,4]{2,1,0:T(2,128)} %param.19) | copy-start | bytes 388
  15.2 13.9 %all-to-all-start = ((s32[2,8,160]{2,0,1:T(2,128)}), s32[2,8,160]{2,0,1:T(2,128)S(1)}, u32[]{:S(2)}, u32[]{:S(2)}) async-start(s32[2,8,160]{2,0,1:T(2,128)} %copy.152), calls=%async_computation | async-start | bytes 32768 | tf_op jit(solution)/shard_map/all_to_all | solution.py:104
  78.0 10.1 %all-to-all-start.1 = ((f32[8,1,1440]{2,1,0:T(1,128)}), f32[8,1,1440]{2,1,0:T(1,128)S(1)}, u32[]{:S(2)}, u32[]{:S(2)}) async-start(f32[8,1,1440]{2,1,0:T(1,128)} %reshape.1452), calls=%async_computation.1 | async-start | bytes 98304 | tf_op jit(solution)/shard_map/all_to_all | solution.py:109
  91.5 7.2 %all-to-all-start.2 = ((f32[4,9,128]{2,1,0:T(8,128)}), f32[4,9,128]{2,1,0:T(8,128)S(1)}, u32[]{:S(2)}, u32[]{:S(2)}) async-start(f32[4,9,128]{2,1,0:T(8,128)} %bitcast.21), calls=%async_computation.2 | async-start | bytes 65536 | tf_op jit(solution)/shard_map/all_to_all | solution.py:161
  94.8 96.0 %all-reduce.8.cloned.1.call-start = ((), (), s32[]{:S(2)}) async-start(), calls=%async_computation.5 | async-start | bytes 262144 | tf_op jit(solution)/shard_map/psum | solution.py:186
  109.6 4.8 %copy-start.8 = (f32[3]{0:T(128)S(1)}, f32[3]{0:T(128)}, u32[]{:S(2)}) copy-start(f32[3]{0:T(128)} %param.20) | copy-start | bytes 40
  149.3 41.5 %copy-start.2 = (f32[3,2048]{1,0:T(4,128)S(1)}, f32[3,2048]{1,0:T(4,128)}, u32[]{:S(2)}) copy-start(f32[3,2048]{1,0:T(4,128)} %param.16) | copy-start | bytes 73732
  149.3 41.5 %copy-start.3 = (f32[3,2048]{1,0:T(4,128)S(1)}, f32[3,2048]{1,0:T(4,128)}, u32[]{:S(2)}) copy-start(f32[3,2048]{1,0:T(4,128)} %param.14) | copy-start | bytes 73732
  149.3 41.4 %copy-start.4 = (f32[3,2048]{1,0:T(4,128)S(1)}, f32[3,2048]{1,0:T(4,128)}, u32[]{:S(2)}) copy-start(f32[3,2048]{1,0:T(4,128)} %param.13) | copy-start | bytes 73732
  149.3 41.4 %copy-start.5 = (f32[10,2048]{1,0:T(8,128)S(1)}, f32[10,2048]{1,0:T(8,128)}, u32[]{:S(2)}) copy-start(f32[10,2048]{1,0:T(8,128)} %param.17) | copy-start | bytes 245764
  149.3 41.4 %copy-start.6 = (f32[10,2048]{1,0:T(8,128)S(1)}, f32[10,2048]{1,0:T(8,128)}, u32[]{:S(2)}) copy-start(f32[10,2048]{1,0:T(8,128)} %param.18) | copy-start | bytes 245764
  149.3 41.4 %copy-start.7 = (f32[1,2048]{1,0:T(1,128)S(1)}, f32[1,2048]{1,0:T(1,128)}, u32[]{:S(2)}) copy-start(f32[1,2048]{1,0:T(1,128)} %param.15) | copy-start | bytes 24580
Sparse Core Ops, SparseCore 0:
  161.1 29.6 all-reduce.7
where the time goes:
time: 200 us; the launch traced here: 199 us
  local copies, waits for them, and re-layouts  62.6 us (31%)
  waiting for transfers between devices  37.7 us (19%)
  other arithmetic  29 us (14%)
  matrix products  20.8 us (10%)
  blocking collectives  20.6 us (10%)
  between operations  14.6 us (7%)
  starting transfers between devices  14.1 us (7%)
    slice x1, local copies, waits for them, and re-layouts, project(): cams[:, 1, 3]  36.3 us
    psum x1, waiting for transfers between devices, body(): gradient = lax.psum(gradient, 'depth')  23.9 us
    dot_general x4, matrix products, running_sum(): jnp.einsum('pbk,kj->pbj', blocks, triangle, precision=lax.Precision.HIGHEST)  17.8 us
    scatter-add x1, other arithmetic, body(): gradient = jnp.zeros_like(params).at[:, rows_in].add(slot_grad)  9.18 us
    all_to_all x1, blocking collectives, body(): lax.all_to_all(outgoing, 'tile', split_axis=1, concat_axis=1, tiled=True)  9.17 us
    all_to_all x1, starting transfers between devices, body(): lax.all_to_all(request, 'tile', split_axis=1, concat_axis=1, tiled=True)  7.31 us
    gather x3, local copies, waits for them, and re-layouts, body(): screen = project(params[:, rows_in], cameras[views_in])  6.92 us
    all_to_all x1, blocking collectives, body(): lax.all_to_all(own_grad, 'depth', split_axis=2, concat_axis=0, tiled=True)  6.22 us
  transfers between devices with their start and end apart: 4, of which 4 were waited for; matrix products, arithmetic and copies ran while one was open for 2% of the time, Pallas kernels for 0%

commit v1 on v0

--- a/solution.py
+++ b/solution.py
@@ -183,7 +183,8 @@
     unused, pullback = jax.vjp(lambda chosen: project(chosen, chosen_cams), params[:, rows_in])
     (slot_grad,) = pullback(incoming.reshape(9, -1))
     gradient = jnp.zeros_like(params).at[:, rows_in].add(slot_grad)
-    gradient = lax.psum(gradient, "depth")
+    parts = lax.all_gather(gradient, "depth")
+    gradient = jnp.sum(parts, axis=0)
     new_params, new_first, new_second = adam_update(params, first_moment, second_moment, gradient)
     return (image, new_params, new_first, new_second)
 

time: 200 us -> 165 us (0.82)
  waiting for transfers between devices: 37.7 us -> 14.7 us
  between operations: 14.6 us -> 1.23 us
  starting transfers between devices: 14.1 us -> 17.4 us
  blocking collectives: 20.6 us -> 18 us
    psum x1 -> x0, waiting for transfers between devices: 23.9 us -> none  [body(): gradient = lax.psum(gradient, 'depth')]
    all_to_all x1 -> x0, blocking collectives: 9.17 us -> none  [body(): lax.all_to_all(outgoing, 'tile', split_axis=1, concat_axis=1, tiled=True)]
    all_gather x0 -> x1, blocking collectives: none -> 6.5 us  [body(): parts = lax.all_gather(gradient, 'depth')]
    all_to_all x0 -> x1, starting transfers between devices: none -> 3.35 us  [body(): lax.all_to_all(outgoing, 'tile', split_axis=1, concat_axis=1, tiled=True)]
    unnamed x29 -> x30, local copies, waits for them, and re-layouts: 4.01 us -> 4.97 us
where the time goes in v1:
time: 165 us; the launch traced here: 163 us
  local copies, waits for them, and re-layouts  62.5 us (38%)
  other arithmetic  28.4 us (17%)
  matrix products  20.9 us (13%)
  blocking collectives  18 us (11%)
  starting transfers between devices  17.4 us (11%)
  waiting for transfers between devices  14.7 us (9%)
    slice x1, local copies, waits for them, and re-layouts, project(): cams[:, 1, 3]  36.3 us
    dot_general x4, matrix products, running_sum(): jnp.einsum('pbk,kj->pbj', blocks, triangle, precision=lax.Precision.HIGHEST)  17.9 us
    scatter-add x1, other arithmetic, body(): gradient = jnp.zeros_like(params).at[:, rows_in].add(slot_grad)  9.18 us
    all_to_all x1, starting transfers between devices, body(): lax.all_to_all(request, 'tile', split_axis=1, concat_axis=1, tiled=True)  7.31 us
    gather x3, local copies, waits for them, and re-layouts, body(): screen = project(params[:, rows_in], cameras[views_in])  6.92 us
    all_gather x1, blocking collectives, body(): parts = lax.all_gather(gradient, 'depth')  6.5 us
    all_to_all x1, blocking collectives, body(): lax.all_to_all(own_grad, 'depth', split_axis=2, concat_axis=0, tiled=True)  6.22 us
    all_to_all x1, waiting for transfers between devices, body(): lax.all_to_all(screen, 'tile', split_axis=1, concat_axis=1, tiled=True)  5.89 us
  transfers between devices with their start and end apart: 4, of which 4 were waited for; matrix products, arithmetic and copies ran while one was open for 2% of the time, Pallas kernels for 0%

profile of v1, /device:TPU:0, one launch (start us, length us, event | category | flops | bytes accessed | tf_op | source)
XLA Modules:
  0.0 163.1 jit_solution(17925172641896074273)
XLA Ops:
  5.8 1.9 %scatter_custom_fusion = s32[2,1280]{0,1:T(8,128)S(1)} fusion(s32[512]{0:T(512)S(1)} %bitcast.199, s32[512,2]{1,0:T(8,128)S(1)} %copy.137, s32[]{:T(128)} %constant.127.clone.1), kind=kCustom, calls=%fused_computation.77 | custom fusion | bytes 10244 | tf_op jit(solution)/shard_map/scatter | solution.py:101
  8.6 7.3 %all-to-all-start = ((s32[2,8,160]{2,0,1:T(2,128)}), s32[2,8,160]{2,0,1:T(2,128)S(1)}, u32[]{:S(2)}, u32[]{:S(2)}) async-start(s32[2,8,160]{2,0,1:T(2,128)} %copy.138), calls=%async_computation | async-start | bytes 32768 | tf_op jit(solution)/shard_map/all_to_all | solution.py:104
  17.8 4.7 %all-to-all-done = s32[2,8,160]{2,0,1:T(2,128)S(1)} async-done(((s32[2,8,160]{2,0,1:T(2,128)}), s32[2,8,160]{2,0,1:T(2,128)S(1)}, u32[]{:S(2)}, u32[]{:S(2)}) %all-to-all-start) | async-done | bytes 10272 | tf_op jit(solution)/shard_map/all_to_all | solution.py:104
  22.7 4.3 %gather_fusion = f32[1280,2,4]{2,1,0:T(2,128)S(1)} fusion(f32[4,2,4]{2,1,0:T(2,128)S(1)} %copy-done.1, s32[2048]{0:T(1024)S(1)} %pad_clamp_fusion.1), kind=kCustom, calls=%fused_computation | custom fusion | bytes 87040 | tf_op jit(solution)/shard_map/gather | solution.py:107
  28.8 36.3 %slice_reduce_fusion = (f32[1280]{0:T(1024)S(1)}, f32[1280]{0:T(1024)S(1)}) fusion(f32[1280,2,4]{2,1,0:T(2,128)S(1)} %gather_fusion), kind=kLoop, calls=%fused_computation.71 | loop fusion | bytes 20480 | tf_op jit(solution)/shard_map/slice | solution.py:15
  66.9 2.4 %gather_fusion.1 = f32[1280,10]{1,0:T(8,128)S(1)} fusion(f32[10,2048]{0,1:T(8,128)S(1)} %copy.140, s32[2048]{0:T(1024)S(1)} %pad_clamp_fusion), kind=kCustom, calls=%fused_computation.1 | custom fusion | bytes 107520 | tf_op jit(solution)/shard_map/gather | solution.py:107
  71.5 3.5 %all-to-all-start.1 = ((f32[8,1,1440]{2,1,0:T(1,128)}), f32[8,1,1440]{2,1,0:T(1,128)S(1)}, u32[]{:S(2)}, u32[]{:S(2)}) async-start(f32[8,1,1440]{2,1,0:T(1,128)} %reshape.1456), calls=%async_computation.1 | async-start | bytes 98304 | tf_op jit(solution)/shard_map/all_to_all | solution.py:109
  75.7 5.9 %all-to-all-done.1 = f32[8,1,1440]{2,1,0:T(1,128)S(1)} async-done(((f32[8,1,1440]{2,1,0:T(1,128)}), f32[8,1,1440]{2,1,0:T(1,128)S(1)}, u32[]{:S(2)}, u32[]{:S(2)}) %all-to-all-start.1) | async-done | bytes 46112 | tf_op jit(solution)/shard_map/all_to_all | solution.py:109
  85.0 3.3 %all-to-all-start.2 = ((f32[4,9,128]{2,1,0:T(8,128)}), f32[4,9,128]{2,1,0:T(8,128)S(1)}, u32[]{:S(2)}, u32[]{:S(2)}) async-start(f32[4,9,128]{2,1,0:T(8,128)} %bitcast.21), calls=%async_computation.2 | async-start | bytes 65536 | tf_op jit(solution)/shard_map/all_to_all | solution.py:161
  88.9 3.3 %all-to-all-done.2 = f32[4,9,128]{2,1,0:T(8,128)S(1)} async-done(((f32[4,9,128]{2,1,0:T(8,128)}), f32[4,9,128]{2,1,0:T(8,128)S(1)}, u32[]{:S(2)}, u32[]{:S(2)}) %all-to-all-start.2) | async-done | bytes 18464 | tf_op jit(solution)/shard_map/all_to_all | solution.py:161
  92.2 2.0 %fusion.28 = f32[1024,4]{0,1:T(4,128)S(1)} fusion(f32[4,128]{1,0:T(4,128)S(1)} %fusion.74, f32[4,128]{1,0:T(4,128)S(1)} %bitcast.167, f32[4,128]{1,0:T(4,128)S(1)} %bitcast.172, f32[1024]{0:T(1024)S(1)} %get-tuple-element.136, f32[4,128]{1,0:T(4,128)S(1)} %broadcast_multiply_fusion.1, f32[4,128]{1,0:T(4,128)S(1)} %bitcast.177, ...), kind=kLoop, calls=%fused_computation.63 | loop fusion | flops 7860224 | bytes 38912 | tf_op jit(solution)/shard_map/while/body/eval_jaxpr/reduce_sum | solution.py:56
  94.2 5.9 %multiply_reduce_fusion.3 = (f32[1024,4]{0,1:T(4,128)S(1)}, f32[1024,4]{0,1:T(4,128)S(1)}, f32[1024,4]{0,1:T(4,128)S(1)}, f32[1024,4,128]{0,2,1:T(8,128)S(1)}, f32[1024,4,128]{0,2,1:T(8,128)}) fusion(f32[4,128]{1,0:T(4,128)S(1)} %bitcast.210, f32[4,128]{1,0:T(4,128)S(1)} %bitcast.190, f32[4,128]{1,0:T(4,128)S(1)} %bitcast.187, f32[1024,4]{0,1:T(4,128)S(1)} %sub.316, ...), kind=kOutput, calls=%fused_computation.60 | convolution fusion | flops 823660544 | bytes 4288512 | tf_op jit(solution)/shard_map/while/body/eval_jaxpr/pbk,kj->pbj/dot_general | solution.py:55
  100.1 2.9 %fusion.24 = f32[1024,4,128]{0,2,1:T(8,128)} fusion(f32[1024,4,128]{0,2,1:T(8,128)S(1)} %get-tuple-element.96, f32[4,128]{1,0:T(4,128)S(1)} %bitcast.191), kind=kOutput, calls=%fused_computation.58 | convolution fusion | flops 805847040 | bytes 4196352 | tf_op jit(solution)/shard_map/while/body/eval_jaxpr/pbk,kj->pbj/dot_general | solution.py:55
  103.0 2.9 %fusion.22 = f32[1024,4,128]{0,2,1:T(8,128)} fusion(f32[1024,4,128]{0,2,1:T(8,128)S(1)} %get-tuple-element.96, f32[4,128]{1,0:T(4,128)S(1)} %bitcast.188), kind=kOutput, calls=%fused_computation.55 | convolution fusion | flops 805847040 | bytes 4196352 | tf_op jit(solution)/shard_map/while/body/eval_jaxpr/pbk,kj->pbj/dot_general | solution.py:55
  105.9 1.9 %fusion.14 = f32[1024]{0:T(1024)S(1)} fusion(f32[512]{0:T(512)S(1)} %fusion.75, f32[512]{0:T(512)S(1)} %bitcast.169, f32[512]{0:T(512)S(1)} %bitcast.174, f32[1024]{0:T(1024)S(1)} %get-tuple-element.136, f32[512]{0:T(512)S(1)} %bitcast.216, f32[512]{0:T(512)S(1)} %bitcast.179, f32[1024]{0:T(1024)S(1)} %get-tuple-element.135, f32[512]{0:T(512)S(1)} %bitcast.184, ...), kind=kLoop, calls=%fused_computation.40 | loop fusion | flops 7863296 | bytes 26624 | tf_op jit(solution)/shard_map/while/body/eval_jaxpr/reduce_sum | solution.py:122
  108.9 1.8 %fusion.56 = f32[3,512]{1,0:T(4,128)S(1)} fusion(f32[1024,512]{0,1:T(8,128)S(1)} %bitcast.143, f32[1,3,1024]{2,1,0:T(4,128)S(1)} %get-tuple-element.129), kind=kOutput, calls=%fused_computation.112 | convolution fusion | flops 18874368 | bytes 2115584 | tf_op jit(solution)/shard_map/while/body/eval_jaxpr/cp,pk->ck/dot_general | solution.py:140
  111.0 6.3 %multiply_multiply_fusion = (f32[1024,4,128]{0,2,1:T(8,128)S(1)}, f32[1024,4,128]{0,2,1:T(8,128)S(1)}) fusion(f32[4,128]{1,0:T(4,128)S(1)} %fusion.74, f32[4,128]{1,0:T(4,128)S(1)} %bitcast.170, f32[4,128]{1,0:T(4,128)S(1)} %bitcast.175, f32[1024]{0:T(1024)S(1)} %get-tuple-element.136, f32[4,128]{1,0:T(4,128)S(1)} %broadcast_multiply_fusion.1, ...), kind=kOutput, calls=%fused_computation.49 | convolution fusion | flops 825245696 | bytes 12701696 | tf_op jit(solution)/shard_map/while/body/eval_jaxpr/pbk,kj->pbj/dot_general | solution.py:55
  117.3 4.1 %fusion.3 = (f32[4,128]{1,0:T(4,128)S(1)}, f32[4,128]{1,0:T(4,128)S(1)}, f32[4,128]{1,0:T(4,128)S(1)}, f32[4,128]{1,0:T(4,128)S(1)}, f32[4,128]{1,0:T(4,128)S(1)}, /*index=5*/f32[4,128]{1,0:T(4,128)S(1)}) fusion(f32[1024,4,128]{0,2,1:T(8,128)S(1)} %get-tuple-element.131, f32[4,128]{1,0:T(4,128)S(1)} %bitcast.164, f32[4,128]{1,0:T(4,128)S(1)} %bitcast.171, ...), kind=kLoop, calls=%fused_computation.29 | loop fusion | flops 17298432 | bytes 4229120 | tf_op jit(solution)/shard_map/while/body/eval_jaxpr/reduce_sum | solution.py:146
  123.2 6.2 %all_to_all.48 = f32[4,1,1152]{2,1,0:T(1,128)S(1)} all-to-all(f32[4,1,1152]{2,1,0:T(1,128)S(1)} %reshape.1458), channel_id=1, replica_groups=mesh['tile'=8,'depth'=4] {'depth'}, dimensions={0} | all-to-all | bytes 36864 | tf_op jit(solution)/shard_map/all_to_all | solution.py:174
  130.8 1.9 %scatter_custom_fusion.1 = f32[9,1280]{0,1:T(8,128)S(1)} fusion(s32[512]{0:T(512)S(1)} %bitcast.201, f32[512,9]{1,0:T(8,128)S(1)} %bitcast.158, f32[]{:T(128)} %constant.132.clone.1), kind=kCustom, calls=%fused_computation.75 | custom fusion | bytes 46084 | tf_op jit(solution)/shard_map/scatter | solution.py:177
  133.8 3.3 %all-to-all-start.4 = ((f32[8,1,1440]{2,1,0:T(1,128)}), f32[8,1,1440]{2,1,0:T(1,128)S(1)}, u32[]{:S(2)}, u32[]{:S(2)}) async-start(f32[8,1,1440]{2,1,0:T(1,128)} %reshape.1460), calls=%async_computation.4 | async-start | bytes 98304 | tf_op jit(solution)/shard_map/all_to_all | solution.py:179
  137.2 5.2 %all-gather.2 = f32[4,3,1024]{2,1,0:T(4,128)S(1)} all-gather(f32[1,3,1024]{2,1,0:T(4,128)S(1)} %get-tuple-element.130), channel_id=2, replica_groups=mesh['tile'=8,'depth'=4] {'depth'}, dimensions={0}, use_global_device_ids=true | all-gather | bytes 61440 | tf_op jit(solution)/shard_map/all_gather | solution.py:175
  146.2 9.2 %scatter_custom_fusion.2 = f32[10,2048]{0,1:T(8,128)S(1)} fusion(s32[1280]{0:T(1024)S(1)} %fusion.60, f32[1280,10]{1,0:T(8,128)S(1)} %copy.164, f32[]{:T(128)} %constant.132.clone.1), kind=kCustom, calls=%fused_computation.73 | custom fusion | flops 12800 | bytes 81924 | tf_op jit(solution)/shard_map/scatter-add | solution.py:185
  155.7 6.5 %all-gather.3 = f32[4,10,2048]{2,1,0:T(8,128)S(1)} all-gather(f32[1,10,2048]{2,1,0:T(8,128)S(1)} %copy.165), channel_id=3, replica_groups=mesh['tile'=8,'depth'=4] {'depth'}, dimensions={0}, use_global_device_ids=true | all-gather | bytes 409600 | tf_op jit(solution)/shard_map/all_gather | solution.py:186
  (127 shorter events, 29.0 us)
Async XLA Ops:
  0.6 15.3 %copy-start = (f32[4,3,1024]{2,0,1:T(4,128)S(1)}, f32[4,3,1024]{2,0,1:T(4,128)}, u32[]{:S(2)}) copy-start(f32[4,3,1024]{2,0,1:T(4,128)} %param.21) | copy-start | bytes 147460
  0.6 16.6 %copy-start.9 = (s32[4]{0:T(128)S(1)}, s32[4]{0:T(128)}, u32[]{:S(2)}) copy-start(s32[4]{0:T(128)} %param.23) | copy-start | bytes 52
  0.7 22.0 %copy-start.1 = (f32[4,2,4]{2,1,0:T(2,128)S(1)}, f32[4,2,4]{2,1,0:T(2,128)}, u32[]{:S(2)}) copy-start(f32[4,2,4]{2,1,0:T(2,128)} %param.19) | copy-start | bytes 388
  8.6 13.9 %all-to-all-start = ((s32[2,8,160]{2,0,1:T(2,128)}), s32[2,8,160]{2,0,1:T(2,128)S(1)}, u32[]{:S(2)}, u32[]{:S(2)}) async-start(s32[2,8,160]{2,0,1:T(2,128)} %copy.138), calls=%async_computation | async-start | bytes 32768 | tf_op jit(solution)/shard_map/all_to_all | solution.py:104
  71.5 10.1 %all-to-all-start.1 = ((f32[8,1,1440]{2,1,0:T(1,128)}), f32[8,1,1440]{2,1,0:T(1,128)S(1)}, u32[]{:S(2)}, u32[]{:S(2)}) async-start(f32[8,1,1440]{2,1,0:T(1,128)} %reshape.1456), calls=%async_computation.1 | async-start | bytes 98304 | tf_op jit(solution)/shard_map/all_to_all | solution.py:109
  85.0 7.2 %all-to-all-start.2 = ((f32[4,9,128]{2,1,0:T(8,128)}), f32[4,9,128]{2,1,0:T(8,128)S(1)}, u32[]{:S(2)}, u32[]{:S(2)}) async-start(f32[4,9,128]{2,1,0:T(8,128)} %bitcast.21), calls=%async_computation.2 | async-start | bytes 65536 | tf_op jit(solution)/shard_map/all_to_all | solution.py:161
  103.0 4.8 %copy-start.8 = (f32[3]{0:T(128)S(1)}, f32[3]{0:T(128)}, u32[]{:S(2)}) copy-start(f32[3]{0:T(128)} %param.20) | copy-start | bytes 40
  133.8 10.1 %all-to-all-start.4 = ((f32[8,1,1440]{2,1,0:T(1,128)}), f32[8,1,1440]{2,1,0:T(1,128)S(1)}, u32[]{:S(2)}, u32[]{:S(2)}) async-start(f32[8,1,1440]{2,1,0:T(1,128)} %reshape.1460), calls=%async_computation.4 | async-start | bytes 98304 | tf_op jit(solution)/shard_map/all_to_all | solution.py:179
  145.8 16.4 %copy-start.2 = (f32[3,2048]{1,0:T(4,128)S(1)}, f32[3,2048]{1,0:T(4,128)}, u32[]{:S(2)}) copy-start(f32[3,2048]{1,0:T(4,128)} %param.16) | copy-start | bytes 73732
  145.8 16.4 %copy-start.3 = (f32[3,2048]{1,0:T(4,128)S(1)}, f32[3,2048]{1,0:T(4,128)}, u32[]{:S(2)}) copy-start(f32[3,2048]{1,0:T(4,128)} %param.14) | copy-start | bytes 73732
  145.8 16.4 %copy-start.4 = (f32[3,2048]{1,0:T(4,128)S(1)}, f32[3,2048]{1,0:T(4,128)}, u32[]{:S(2)}) copy-start(f32[3,2048]{1,0:T(4,128)} %param.13) | copy-start | bytes 73732
  145.9 16.4 %copy-start.5 = (f32[10,2048]{1,0:T(8,128)S(1)}, f32[10,2048]{1,0:T(8,128)}, u32[]{:S(2)}) copy-start(f32[10,2048]{1,0:T(8,128)} %param.17) | copy-start | bytes 245764
  145.9 16.4 %copy-start.6 = (f32[10,2048]{1,0:T(8,128)S(1)}, f32[10,2048]{1,0:T(8,128)}, u32[]{:S(2)}) copy-start(f32[10,2048]{1,0:T(8,128)} %param.18) | copy-start | bytes 245764
  145.9 16.4 %copy-start.7 = (f32[1,2048]{1,0:T(1,128)S(1)}, f32[1,2048]{1,0:T(1,128)}, u32[]{:S(2)}) copy-start(f32[1,2048]{1,0:T(1,128)} %param.15) | copy-start | bytes 24580
